TPU v7x, 32 devices: a whole 2x2x4 slice. The times are simulated.
32 devices in a mesh: section: 4 (over x, core), obs: 8 (over z, y).
Axes of the slice: x: 2, y: 2, z: 4, core: 2. Of those that a mesh axis runs over, the one named last changes fastest.
Arguments:
- predictors: bfloat16 [4, 4, 20, 32768], P('section', None, None, 'obs'), may hold values from -5 to 5
- departures: float32 [4, 4, 32768], P('section', None, 'obs'), may hold values from -30 to 30
- obs_precision: float32 [4, 4, 32768], P('section', None, 'obs'), may hold values from 0.3 to 3
- qc_pass: int32 [4, 4, 32768], P('section', None, 'obs'), may hold values 0 or 1
- block_channel: int32 [4, 4, 256], P('section', None, 'obs'), may hold values from 0 to 2047, as said below
- stream_order: int32 [4], replicated, may hold values from 0 to 3, each once
- prior_coeffs: float32 [4, 20, 2048], P(None, None, 'obs'), may hold values from -1 to 1
- prior_info: float32 [4, 210, 2048], P(None, None, 'obs'), may hold values from -1 to 32, as said below
- memory_factor: float32 [2048], P('obs'), may hold values from 0.5 to 0.98
Outputs:
- coeffs: float32 [4, 4, 20, 2048], P('section', None, None, 'obs')
- information: float32 [4, 4, 210, 2048], P('section', None, None, 'obs')
Inputs may be any that keep to these rules, and one draw needn't show every extreme that they name: `block_channel`: among the 32 row blocks of one index of obs, at most 8 have channels in any one range of the 256 channels from a multiple of 256; in every window and stream one such range holds exactly 8 blocks of every index of obs. `stream_order`: each stream appears once. `prior_info`: for every stream and channel the 210 entries are the upper triangle, row by row, of a symmetric positive definite matrix of order 20.
All inputs are finite; a program needn't handle non-finite values. No bound on the sum of `qc_pass` on one device may be relied on, other than what follows from the above.
Results may differ from a plain program's by a relative error of at most 0.0038.
Values sent between devices are 32-bit elements; how exact they have to be, the bound alone decides.
A program may use at most 64 MiB of HBM per device.

v0:
```python
import jax
import jax.numpy as jnp
import numpy as np
from jax import lax
from jax.sharding import PartitionSpec as P

HUBER_SQ = 9.0
PRIOR_WEIGHT = 64.0


def from_behind(array, axis, by):
    size = lax.axis_size(axis)
    pairs = [(i, i + by) for i in range(size) if 0 <= i + by < size]
    return lax.ppermute(array, axis, pairs)


def upper_positions(dimension):
    return np.array(
        [i * dimension + j for i in range(dimension) for j in range(i, dimension)], dtype=np.int32
    )


def solve_packed(packed, target):
    dimension = target.shape[0]
    placing = {}
    counter = 0
    for i in range(dimension):
        for j in range(i, dimension):
            placing[i, j] = counter
            counter += 1
    factor = [[None] * dimension for i in range(dimension)]
    for j in range(dimension):
        pivot_root = jnp.sqrt(
            packed[placing[j, j]] - sum((factor[j][k] * factor[j][k] for k in range(j)))
        )
        factor[j][j] = pivot_root
        for i in range(j + 1, dimension):
            factor[i][j] = (
                packed[placing[j, i]] - sum((factor[i][k] * factor[j][k] for k in range(j)))
            ) / pivot_root
    forward = []
    for i in range(dimension):
        forward.append(
            (target[i] - sum((factor[i][k] * forward[k] for k in range(i)))) / factor[i][i]
        )
    backward = [None] * dimension
    for i in reversed(range(dimension)):
        backward[i] = (
            forward[i] - sum((factor[k][i] * backward[k] for k in range(i + 1, dimension)))
        ) / factor[i][i]
    return jnp.stack(backward)


def block_terms(predicted, departed, precision, passed, block_coeffs):
    pred_count, row_count = predicted.shape
    block_count = block_coeffs.shape[1]
    block_width = row_count // block_count
    upper_index = upper_positions(pred_count)
    shaped = predicted.reshape(pred_count, block_count, block_width)
    offset = jnp.sum(shaped.astype(jnp.float32) * block_coeffs[:, :, None], axis=0)
    residual = departed.reshape(block_count, block_width) - offset
    scale_row = precision.reshape(block_count, block_width)
    weight = (
        passed.reshape(block_count, block_width).astype(jnp.float32)
        * scale_row
        / (1.0 + scale_row * residual * residual / HUBER_SQ)
    )
    weighted = (weight[None] * shaped.astype(jnp.float32)).astype(jnp.bfloat16)
    chi_square = jnp.sum(weight * residual * residual)
    passed_count = jnp.sum(passed.astype(jnp.float32))
    gram_full = lax.dot_general(
        weighted, shaped, (((2,), (2,)), ((1,), (1,))), preferred_element_type=jnp.float32
    )
    gram_upper = gram_full.reshape(block_count, pred_count * pred_count)[:, upper_index]
    gradient = jnp.sum(weighted.astype(jnp.float32) * residual[None], axis=2).T
    return (jnp.concatenate([gram_upper, gradient], axis=1), jnp.stack([chi_square, passed_count]))


def local(
    predictors,
    departures,
    obs_precision,
    qc_pass,
    block_channel,
    stream_order,
    prior_coeffs,
    prior_info,
    memory_factor,
):
    section_count = lax.axis_size("section")
    obs_devices = lax.axis_size("obs")
    section_place = lax.axis_index("section")
    stream_count = stream_order.shape[0]
    local_channels = memory_factor.shape[0]
    block_count = block_channel.shape[2]
    pred_count = prior_coeffs.shape[1]
    tri_count = prior_info.shape[1]
    column_count = tri_count + pred_count
    capacity = 2 * block_count // obs_devices
    local_line = jnp.arange(local_channels, dtype=jnp.float32)
    owner_line = jnp.arange(obs_devices, dtype=jnp.int32)
    slot_line = jnp.arange(obs_devices * capacity, dtype=jnp.int32)
    highest = lax.Precision.HIGHEST

    def pack_blocks(block_sums, channel):
        owner_index = channel // local_channels
        inner_channel = channel % local_channels
        owner_hot = (owner_index[:, None] == owner_line[None, :]).astype(jnp.int32)
        ranking = jnp.sum((jnp.cumsum(owner_hot, axis=0) - 1) * owner_hot, axis=1)
        slot_of = owner_index * capacity + ranking
        placing = (slot_of[:, None] == slot_line[None, :]).astype(jnp.float32)
        send_rows = lax.dot_general(
            placing,
            block_sums,
            (((0,), (0,)), ((), ())),
            precision=highest,
            preferred_element_type=jnp.float32,
        ).reshape(obs_devices, capacity, column_count)
        send_channel = (
            lax.dot_general(
                placing,
                (inner_channel + 1).astype(jnp.float32),
                (((0,), (0,)), ((), ())),
                precision=highest,
                preferred_element_type=jnp.float32,
            ).reshape(obs_devices, capacity)
            - 1.0
        )
        return (send_rows, send_channel)

    def unpack_blocks(got_rows, got_channel):
        gather_hot = (got_channel.reshape(-1)[:, None] == local_line[None, :]).astype(jnp.float32)
        return lax.dot_general(
            got_rows.reshape(-1, column_count),
            gather_hot,
            (((0,), (0,)), ((), ())),
            precision=highest,
            preferred_element_type=jnp.float32,
        )

    def window_work(state_now, streams):
        beta_prior = state_now[:, :pred_count]
        info_prior = state_now[:, pred_count:]
        all_coeffs = lax.all_gather(beta_prior, "obs", axis=2, tiled=True)
        channel = jnp.take(block_channel[0], streams, axis=0)
        block_coeffs = jax.vmap(lambda coeff_rows, chan: jnp.take(coeff_rows, chan, axis=1))(
            all_coeffs, channel
        )
        block_sums, statistics = jax.vmap(block_terms)(
            jnp.take(predictors[0], streams, axis=0),
            jnp.take(departures[0], streams, axis=0),
            jnp.take(obs_precision[0], streams, axis=0),
            jnp.take(qc_pass[0], streams, axis=0),
            block_coeffs,
        )
        totals = lax.psum(statistics, "obs")
        send_rows, send_channel = jax.vmap(pack_blocks)(block_sums, channel)
        got_rows, got_channel = (
            lax.all_to_all(send_rows, "obs", split_axis=1, concat_axis=1, tiled=True),
            lax.all_to_all(send_channel, "obs", split_axis=1, concat_axis=1, tiled=True),
        )
        normal = jax.vmap(unpack_blocks)(got_rows, got_channel)
        inflation = (totals[:, 0] + PRIOR_WEIGHT) / (totals[:, 1] + PRIOR_WEIGHT)
        info_post = info_prior + normal[:, :tri_count] / inflation[:, None, None]
        beta_post = beta_prior + jax.vmap(solve_packed)(
            info_post, normal[:, tri_count:] / inflation[:, None, None]
        )
        outgoing = jnp.concatenate([beta_post, memory_factor[None, None, :] * info_post], axis=1)
        incoming = from_behind(outgoing, "section", 1)
        return (beta_post, info_post, incoming)

    def fresh_of(streams):
        return jnp.concatenate(
            [jnp.take(prior_coeffs, streams, axis=0), jnp.take(prior_info, streams, axis=0)], axis=1
        )

    coeff_start = jnp.zeros((1, stream_count, pred_count, local_channels), jnp.float32)
    info_start = jnp.zeros((1, stream_count, tri_count, local_channels), jnp.float32)

    def tick_step(t, loop_state):
        incoming, coeff_out, info_out = loop_state
        entry_index = t - section_place
        usable = (entry_index >= 0) & (entry_index < stream_count)
        slot_index = jnp.clip(entry_index, 0, stream_count - 1)
        streams = lax.dynamic_slice_in_dim(stream_order, slot_index, 1, 0)
        state_now = jnp.where(
            (section_place == 0) | jnp.logical_not(usable), fresh_of(streams), incoming
        )
        beta_post, info_post, incoming = window_work(state_now, streams)

        def store_entry(buffer, result):
            current = lax.dynamic_slice_in_dim(buffer, slot_index, 1, 1)
            updated = jnp.where(usable, result[None], current)
            return lax.dynamic_update_slice_in_dim(buffer, updated, slot_index, 1)

        return (incoming, store_entry(coeff_out, beta_post), store_entry(info_out, info_post))

    initial = (jnp.zeros((1, column_count, local_channels), jnp.float32), coeff_start, info_start)
    final_state = lax.fori_loop(0, stream_count + section_count - 1, tick_step, initial)
    return (final_state[1], final_state[2])


def solution(mesh):
    in_specs = (
        P("section", None, None, "obs"),
        P("section", None, "obs"),
        P("section", None, "obs"),
        P("section", None, "obs"),
        P("section", None, "obs"),
        P(),
        P(None, None, "obs"),
        P(None, None, "obs"),
        P("obs"),
    )
    out_specs = (P("section", None, None, "obs"), P("section", None, None, "obs"))
    return jax.shard_map(local, mesh=mesh, in_specs=in_specs, out_specs=out_specs, check_vma=False)
```

profile of v0, /device:TPU:1, one launch (start us, length us, event | category | flops | bytes accessed | tf_op | source)
XLA Modules:
  0.0 688.5 jit_solution(5905409147109336993)
XLA Ops:
  2.9 684.6 %while.38 = (s32[]{:T(128)}, f32[1,230,256]{2,1,0:T(8,128)S(1)}, f32[1,4,20,256]{3,1,2,0:T(4,128)S(1)}, f32[1,4,210,256]{3,1,2,0:T(4,128)S(1)}, s32[]{:T(128)}, ...) while((s32[]{:T(128)}, f32[1,230,256]{2,1,0:T(8,128)S(1)}, ...), condition=%wide.region_8.10_spmd.clone.clone, body=%wide.region_0.9_spmd.sunk.clone.clone.sunk | while | flops 57759508 | bytes 13853709 | solution.py:199
  7.5 6.4 all-to-all-start.1
  16.3 24.6 %all_gather.15 = f32[1,20,2048]{2,1,0:T(8,128)S(1)} all-gather(f32[1,20,256]{2,1,0:T(8,128)S(1)} %slice.5342), channel_id=1, replica_groups=mesh['section'=4,'obs'=8] {'obs'}, dimensions={2}, use_global_device_ids=true | all-gather | bytes 184320 | tf_op jit(solution)/shard_map/while/body/eval_jaxpr/all_gather | solution.py:144
  47.6 17.5 %psum.19 = f32[1,2]{1,0:T(1,128)S(1)} all-reduce(f32[1,2]{1,0:T(1,128)S(1)} %maximum_bitcast_fusion.6), channel_id=1, replica_groups=mesh['section'=4,'obs'=8] {'obs'}, use_global_device_ids=true, to_apply=%region_7.8 | all-reduce | flops 2 | bytes 16 | tf_op jit(solution)/shard_map/while/body/eval_jaxpr/psum | solution.py:156
  72.6 4.4 all-to-all-done
  83.2 15.7 %collective-permute-start = (f32[1,230,256]{2,1,0:T(8,128)S(1)}, f32[1,230,256]{2,1,0:T(8,128)S(1)}, u32[]{:S(2)}, u32[]{:S(2)}) collective-permute-start(f32[1,230,256]{2,1,0:T(8,128)S(1)} %pad_maximum_fusion.2), channel_id=1, source_target_pairs={{0,8},{8,16},{16,24},{1,9},{9,17},{17,25},{2,10},{10,18},{18,26},{... | collective-permute-start | bytes 706568 | tf_op jit(solution)/shard_map/while/body/eval_jaxpr/ppermute | solution.py:14
  99.3 5.9 dynamic_update_slice.31
  115.6 25.2 %all_gather.15 = f32[1,20,2048]{2,1,0:T(8,128)S(1)} all-gather(f32[1,20,256]{2,1,0:T(8,128)S(1)} %slice.5342), channel_id=1, replica_groups=mesh['section'=4,'obs'=8] {'obs'}, dimensions={2}, use_global_device_ids=true | all-gather | bytes 184320 | tf_op jit(solution)/shard_map/while/body/eval_jaxpr/all_gather | solution.py:144
  147.5 17.3 %psum.19 = f32[1,2]{1,0:T(1,128)S(1)} all-reduce(f32[1,2]{1,0:T(1,128)S(1)} %maximum_bitcast_fusion.6), channel_id=1, replica_groups=mesh['section'=4,'obs'=8] {'obs'}, use_global_device_ids=true, to_apply=%region_7.8 | all-reduce | flops 2 | bytes 16 | tf_op jit(solution)/shard_map/while/body/eval_jaxpr/psum | solution.py:156
  172.3 4.4 all-to-all-done
  182.9 13.1 %collective-permute-start = (f32[1,230,256]{2,1,0:T(8,128)S(1)}, f32[1,230,256]{2,1,0:T(8,128)S(1)}, u32[]{:S(2)}, u32[]{:S(2)}) collective-permute-start(f32[1,230,256]{2,1,0:T(8,128)S(1)} %pad_maximum_fusion.2), channel_id=1, source_target_pairs={{0,8},{8,16},{16,24},{1,9},{9,17},{17,25},{2,10},{10,18},{18,26},{... | collective-permute-start | bytes 706568 | tf_op jit(solution)/shard_map/while/body/eval_jaxpr/ppermute | solution.py:14
  196.4 5.9 dynamic_update_slice.31
  212.6 24.6 %all_gather.15 = f32[1,20,2048]{2,1,0:T(8,128)S(1)} all-gather(f32[1,20,256]{2,1,0:T(8,128)S(1)} %slice.5342), channel_id=1, replica_groups=mesh['section'=4,'obs'=8] {'obs'}, dimensions={2}, use_global_device_ids=true | all-gather | bytes 184320 | tf_op jit(solution)/shard_map/while/body/eval_jaxpr/all_gather | solution.py:144
  244.0 17.5 %psum.19 = f32[1,2]{1,0:T(1,128)S(1)} all-reduce(f32[1,2]{1,0:T(1,128)S(1)} %maximum_bitcast_fusion.6), channel_id=1, replica_groups=mesh['section'=4,'obs'=8] {'obs'}, use_global_device_ids=true, to_apply=%region_7.8 | all-reduce | flops 2 | bytes 16 | tf_op jit(solution)/shard_map/while/body/eval_jaxpr/psum | solution.py:156
  279.6 13.4 %collective-permute-start = (f32[1,230,256]{2,1,0:T(8,128)S(1)}, f32[1,230,256]{2,1,0:T(8,128)S(1)}, u32[]{:S(2)}, u32[]{:S(2)}) collective-permute-start(f32[1,230,256]{2,1,0:T(8,128)S(1)} %pad_maximum_fusion.2), channel_id=1, source_target_pairs={{0,8},{8,16},{16,24},{1,9},{9,17},{17,25},{2,10},{10,18},{18,26},{... | collective-permute-start | bytes 706568 | tf_op jit(solution)/shard_map/while/body/eval_jaxpr/ppermute | solution.py:14
  293.4 5.9 dynamic_update_slice.31
  309.7 24.8 %all_gather.15 = f32[1,20,2048]{2,1,0:T(8,128)S(1)} all-gather(f32[1,20,256]{2,1,0:T(8,128)S(1)} %slice.5342), channel_id=1, replica_groups=mesh['section'=4,'obs'=8] {'obs'}, dimensions={2}, use_global_device_ids=true | all-gather | bytes 184320 | tf_op jit(solution)/shard_map/while/body/eval_jaxpr/all_gather | solution.py:144
  341.3 17.6 %psum.19 = f32[1,2]{1,0:T(1,128)S(1)} all-reduce(f32[1,2]{1,0:T(1,128)S(1)} %maximum_bitcast_fusion.6), channel_id=1, replica_groups=mesh['section'=4,'obs'=8] {'obs'}, use_global_device_ids=true, to_apply=%region_7.8 | all-reduce | flops 2 | bytes 16 | tf_op jit(solution)/shard_map/while/body/eval_jaxpr/psum | solution.py:156
  377.0 13.1 %collective-permute-start = (f32[1,230,256]{2,1,0:T(8,128)S(1)}, f32[1,230,256]{2,1,0:T(8,128)S(1)}, u32[]{:S(2)}, u32[]{:S(2)}) collective-permute-start(f32[1,230,256]{2,1,0:T(8,128)S(1)} %pad_maximum_fusion.2), channel_id=1, source_target_pairs={{0,8},{8,16},{16,24},{1,9},{9,17},{17,25},{2,10},{10,18},{18,26},{... | collective-permute-start | bytes 706568 | tf_op jit(solution)/shard_map/while/body/eval_jaxpr/ppermute | solution.py:14
  390.5 5.9 dynamic_update_slice.31
  406.7 24.9 %all_gather.15 = f32[1,20,2048]{2,1,0:T(8,128)S(1)} all-gather(f32[1,20,256]{2,1,0:T(8,128)S(1)} %slice.5342), channel_id=1, replica_groups=mesh['section'=4,'obs'=8] {'obs'}, dimensions={2}, use_global_device_ids=true | all-gather | bytes 184320 | tf_op jit(solution)/shard_map/while/body/eval_jaxpr/all_gather | solution.py:144
  438.4 17.2 %psum.19 = f32[1,2]{1,0:T(1,128)S(1)} all-reduce(f32[1,2]{1,0:T(1,128)S(1)} %maximum_bitcast_fusion.6), channel_id=1, replica_groups=mesh['section'=4,'obs'=8] {'obs'}, use_global_device_ids=true, to_apply=%region_7.8 | all-reduce | flops 2 | bytes 16 | tf_op jit(solution)/shard_map/while/body/eval_jaxpr/psum | solution.py:156
  473.8 13.4 %collective-permute-start = (f32[1,230,256]{2,1,0:T(8,128)S(1)}, f32[1,230,256]{2,1,0:T(8,128)S(1)}, u32[]{:S(2)}, u32[]{:S(2)}) collective-permute-start(f32[1,230,256]{2,1,0:T(8,128)S(1)} %pad_maximum_fusion.2), channel_id=1, source_target_pairs={{0,8},{8,16},{16,24},{1,9},{9,17},{17,25},{2,10},{10,18},{18,26},{... | collective-permute-start | bytes 706568 | tf_op jit(solution)/shard_map/while/body/eval_jaxpr/ppermute | solution.py:14
  487.5 5.9 dynamic_update_slice.31
  503.8 24.8 %all_gather.15 = f32[1,20,2048]{2,1,0:T(8,128)S(1)} all-gather(f32[1,20,256]{2,1,0:T(8,128)S(1)} %slice.5342), channel_id=1, replica_groups=mesh['section'=4,'obs'=8] {'obs'}, dimensions={2}, use_global_device_ids=true | all-gather | bytes 184320 | tf_op jit(solution)/shard_map/while/body/eval_jaxpr/all_gather | solution.py:144
  535.4 17.5 %psum.19 = f32[1,2]{1,0:T(1,128)S(1)} all-reduce(f32[1,2]{1,0:T(1,128)S(1)} %maximum_bitcast_fusion.6), channel_id=1, replica_groups=mesh['section'=4,'obs'=8] {'obs'}, use_global_device_ids=true, to_apply=%region_7.8 | all-reduce | flops 2 | bytes 16 | tf_op jit(solution)/shard_map/while/body/eval_jaxpr/psum | solution.py:156
  571.0 13.2 %collective-permute-start = (f32[1,230,256]{2,1,0:T(8,128)S(1)}, f32[1,230,256]{2,1,0:T(8,128)S(1)}, u32[]{:S(2)}, u32[]{:S(2)}) collective-permute-start(f32[1,230,256]{2,1,0:T(8,128)S(1)} %pad_maximum_fusion.2), channel_id=1, source_target_pairs={{0,8},{8,16},{16,24},{1,9},{9,17},{17,25},{2,10},{10,18},{18,26},{... | collective-permute-start | bytes 706568 | tf_op jit(solution)/shard_map/while/body/eval_jaxpr/ppermute | solution.py:14
  584.6 5.9 dynamic_update_slice.31
  600.9 24.5 %all_gather.15 = f32[1,20,2048]{2,1,0:T(8,128)S(1)} all-gather(f32[1,20,256]{2,1,0:T(8,128)S(1)} %slice.5342), channel_id=1, replica_groups=mesh['section'=4,'obs'=8] {'obs'}, dimensions={2}, use_global_device_ids=true | all-gather | bytes 184320 | tf_op jit(solution)/shard_map/while/body/eval_jaxpr/all_gather | solution.py:144
  632.1 18.0 %psum.19 = f32[1,2]{1,0:T(1,128)S(1)} all-reduce(f32[1,2]{1,0:T(1,128)S(1)} %maximum_bitcast_fusion.6), channel_id=1, replica_groups=mesh['section'=4,'obs'=8] {'obs'}, use_global_device_ids=true, to_apply=%region_7.8 | all-reduce | flops 2 | bytes 16 | tf_op jit(solution)/shard_map/while/body/eval_jaxpr/psum | solution.py:156
  668.2 13.1 %collective-permute-start = (f32[1,230,256]{2,1,0:T(8,128)S(1)}, f32[1,230,256]{2,1,0:T(8,128)S(1)}, u32[]{:S(2)}, u32[]{:S(2)}) collective-permute-start(f32[1,230,256]{2,1,0:T(8,128)S(1)} %pad_maximum_fusion.2), channel_id=1, source_target_pairs={{0,8},{8,16},{16,24},{1,9},{9,17},{17,25},{2,10},{10,18},{18,26},{... | collective-permute-start | bytes 706568 | tf_op jit(solution)/shard_map/while/body/eval_jaxpr/ppermute | solution.py:14
  681.7 5.9 dynamic_update_slice.31
  (648 shorter events, 214.5 us)
Async XLA Ops:
  2.2 0.7 copy-start.4
  2.3 0.7 copy-start.5
  7.5 60.4 %all-to-all-start.1 = ((f32[1,8,8]{2,0,1:T(1,128)}), f32[1,8,8]{2,0,1:T(1,128)S(1)}, u32[]{:S(2)}, u32[]{:S(2)}) async-start(f32[1,8,8]{2,0,1:T(1,128)} %bitcast.2454), calls=%async_computation.1 | async-start | bytes 8192 | tf_op jit(solution)/shard_map/while/body/eval_jaxpr/all_to_all | solution.py:160
  68.0 9.1 %all-to-all-start = ((f32[1,8,8,230]{3,2,0,1:T(8,128)}), f32[1,8,8,230]{3,2,0,1:T(8,128)S(1)}, u32[]{:S(2)}, u32[]{:S(2)}) async-start(f32[1,8,8,230]{3,2,0,1:T(8,128)} %convolution_bitcast_fusion.4), calls=%async_computation | async-start | bytes 131072 | tf_op jit(solution)/shard_map/while/body/eval_jaxpr/all_to_all | solution.py:159
  80.7 0.7 copy-start.1
  83.2 22.0 %collective-permute-start = (f32[1,230,256]{2,1,0:T(8,128)S(1)}, f32[1,230,256]{2,1,0:T(8,128)S(1)}, u32[]{:S(2)}, u32[]{:S(2)}) collective-permute-start(f32[1,230,256]{2,1,0:T(8,128)S(1)} %pad_maximum_fusion.2), channel_id=1, source_target_pairs={{0,8},{8,16},{16,24},{1,9},{9,17},{17,25},{2,10},{10,18},{18,26},{... | collective-permute-start | bytes 706568 | tf_op jit(solution)/shard_map/while/body/eval_jaxpr/ppermute | solution.py:14
  109.8 57.8 %all-to-all-start.1 = ((f32[1,8,8]{2,0,1:T(1,128)}), f32[1,8,8]{2,0,1:T(1,128)S(1)}, u32[]{:S(2)}, u32[]{:S(2)}) async-start(f32[1,8,8]{2,0,1:T(1,128)} %bitcast.2454), calls=%async_computation.1 | async-start | bytes 8192 | tf_op jit(solution)/shard_map/while/body/eval_jaxpr/all_to_all | solution.py:160
  167.6 9.1 %all-to-all-start = ((f32[1,8,8,230]{3,2,0,1:T(8,128)}), f32[1,8,8,230]{3,2,0,1:T(8,128)S(1)}, u32[]{:S(2)}, u32[]{:S(2)}) async-start(f32[1,8,8,230]{3,2,0,1:T(8,128)} %convolution_bitcast_fusion.4), calls=%async_computation | async-start | bytes 131072 | tf_op jit(solution)/shard_map/while/body/eval_jaxpr/all_to_all | solution.py:159
  180.4 0.7 copy-start.1
  182.9 19.4 %collective-permute-start = (f32[1,230,256]{2,1,0:T(8,128)S(1)}, f32[1,230,256]{2,1,0:T(8,128)S(1)}, u32[]{:S(2)}, u32[]{:S(2)}) collective-permute-start(f32[1,230,256]{2,1,0:T(8,128)S(1)} %pad_maximum_fusion.2), channel_id=1, source_target_pairs={{0,8},{8,16},{16,24},{1,9},{9,17},{17,25},{2,10},{10,18},{18,26},{... | collective-permute-start | bytes 706568 | tf_op jit(solution)/shard_map/while/body/eval_jaxpr/ppermute | solution.py:14
  206.9 57.5 %all-to-all-start.1 = ((f32[1,8,8]{2,0,1:T(1,128)}), f32[1,8,8]{2,0,1:T(1,128)S(1)}, u32[]{:S(2)}, u32[]{:S(2)}) async-start(f32[1,8,8]{2,0,1:T(1,128)} %bitcast.2454), calls=%async_computation.1 | async-start | bytes 8192 | tf_op jit(solution)/shard_map/while/body/eval_jaxpr/all_to_all | solution.py:160
  264.4 9.1 %all-to-all-start = ((f32[1,8,8,230]{3,2,0,1:T(8,128)}), f32[1,8,8,230]{3,2,0,1:T(8,128)S(1)}, u32[]{:S(2)}, u32[]{:S(2)}) async-start(f32[1,8,8,230]{3,2,0,1:T(8,128)} %convolution_bitcast_fusion.4), calls=%async_computation | async-start | bytes 131072 | tf_op jit(solution)/shard_map/while/body/eval_jaxpr/all_to_all | solution.py:159
  277.1 0.7 copy-start.1
  279.6 19.7 %collective-permute-start = (f32[1,230,256]{2,1,0:T(8,128)S(1)}, f32[1,230,256]{2,1,0:T(8,128)S(1)}, u32[]{:S(2)}, u32[]{:S(2)}) collective-permute-start(f32[1,230,256]{2,1,0:T(8,128)S(1)} %pad_maximum_fusion.2), channel_id=1, source_target_pairs={{0,8},{8,16},{16,24},{1,9},{9,17},{17,25},{2,10},{10,18},{18,26},{... | collective-permute-start | bytes 706568 | tf_op jit(solution)/shard_map/while/body/eval_jaxpr/ppermute | solution.py:14
  303.9 57.8 %all-to-all-start.1 = ((f32[1,8,8]{2,0,1:T(1,128)}), f32[1,8,8]{2,0,1:T(1,128)S(1)}, u32[]{:S(2)}, u32[]{:S(2)}) async-start(f32[1,8,8]{2,0,1:T(1,128)} %bitcast.2454), calls=%async_computation.1 | async-start | bytes 8192 | tf_op jit(solution)/shard_map/while/body/eval_jaxpr/all_to_all | solution.py:160
  361.8 9.1 %all-to-all-start = ((f32[1,8,8,230]{3,2,0,1:T(8,128)}), f32[1,8,8,230]{3,2,0,1:T(8,128)S(1)}, u32[]{:S(2)}, u32[]{:S(2)}) async-start(f32[1,8,8,230]{3,2,0,1:T(8,128)} %convolution_bitcast_fusion.4), calls=%async_computation | async-start | bytes 131072 | tf_op jit(solution)/shard_map/while/body/eval_jaxpr/all_to_all | solution.py:159
  374.5 0.7 copy-start.1
  377.0 19.4 %collective-permute-start = (f32[1,230,256]{2,1,0:T(8,128)S(1)}, f32[1,230,256]{2,1,0:T(8,128)S(1)}, u32[]{:S(2)}, u32[]{:S(2)}) collective-permute-start(f32[1,230,256]{2,1,0:T(8,128)S(1)} %pad_maximum_fusion.2), channel_id=1, source_target_pairs={{0,8},{8,16},{16,24},{1,9},{9,17},{17,25},{2,10},{10,18},{18,26},{... | collective-permute-start | bytes 706568 | tf_op jit(solution)/shard_map/while/body/eval_jaxpr/ppermute | solution.py:14
  401.0 57.5 %all-to-all-start.1 = ((f32[1,8,8]{2,0,1:T(1,128)}), f32[1,8,8]{2,0,1:T(1,128)S(1)}, u32[]{:S(2)}, u32[]{:S(2)}) async-start(f32[1,8,8]{2,0,1:T(1,128)} %bitcast.2454), calls=%async_computation.1 | async-start | bytes 8192 | tf_op jit(solution)/shard_map/while/body/eval_jaxpr/all_to_all | solution.py:160
  458.5 9.1 %all-to-all-start = ((f32[1,8,8,230]{3,2,0,1:T(8,128)}), f32[1,8,8,230]{3,2,0,1:T(8,128)S(1)}, u32[]{:S(2)}, u32[]{:S(2)}) async-start(f32[1,8,8,230]{3,2,0,1:T(8,128)} %convolution_bitcast_fusion.4), calls=%async_computation | async-start | bytes 131072 | tf_op jit(solution)/shard_map/while/body/eval_jaxpr/all_to_all | solution.py:159
  471.3 0.7 copy-start.1
  473.8 19.7 %collective-permute-start = (f32[1,230,256]{2,1,0:T(8,128)S(1)}, f32[1,230,256]{2,1,0:T(8,128)S(1)}, u32[]{:S(2)}, u32[]{:S(2)}) collective-permute-start(f32[1,230,256]{2,1,0:T(8,128)S(1)} %pad_maximum_fusion.2), channel_id=1, source_target_pairs={{0,8},{8,16},{16,24},{1,9},{9,17},{17,25},{2,10},{10,18},{18,26},{... | collective-permute-start | bytes 706568 | tf_op jit(solution)/shard_map/while/body/eval_jaxpr/ppermute | solution.py:14
  498.1 57.7 %all-to-all-start.1 = ((f32[1,8,8]{2,0,1:T(1,128)}), f32[1,8,8]{2,0,1:T(1,128)S(1)}, u32[]{:S(2)}, u32[]{:S(2)}) async-start(f32[1,8,8]{2,0,1:T(1,128)} %bitcast.2454), calls=%async_computation.1 | async-start | bytes 8192 | tf_op jit(solution)/shard_map/while/body/eval_jaxpr/all_to_all | solution.py:160
  555.8 9.1 %all-to-all-start = ((f32[1,8,8,230]{3,2,0,1:T(8,128)}), f32[1,8,8,230]{3,2,0,1:T(8,128)S(1)}, u32[]{:S(2)}, u32[]{:S(2)}) async-start(f32[1,8,8,230]{3,2,0,1:T(8,128)} %convolution_bitcast_fusion.4), calls=%async_computation | async-start | bytes 131072 | tf_op jit(solution)/shard_map/while/body/eval_jaxpr/all_to_all | solution.py:159
  568.5 0.7 copy-start.1
  571.0 19.5 %collective-permute-start = (f32[1,230,256]{2,1,0:T(8,128)S(1)}, f32[1,230,256]{2,1,0:T(8,128)S(1)}, u32[]{:S(2)}, u32[]{:S(2)}) collective-permute-start(f32[1,230,256]{2,1,0:T(8,128)S(1)} %pad_maximum_fusion.2), channel_id=1, source_target_pairs={{0,8},{8,16},{16,24},{1,9},{9,17},{17,25},{2,10},{10,18},{18,26},{... | collective-permute-start | bytes 706568 | tf_op jit(solution)/shard_map/while/body/eval_jaxpr/ppermute | solution.py:14
  595.1 57.8 %all-to-all-start.1 = ((f32[1,8,8]{2,0,1:T(1,128)}), f32[1,8,8]{2,0,1:T(1,128)S(1)}, u32[]{:S(2)}, u32[]{:S(2)}) async-start(f32[1,8,8]{2,0,1:T(1,128)} %bitcast.2454), calls=%async_computation.1 | async-start | bytes 8192 | tf_op jit(solution)/shard_map/while/body/eval_jaxpr/all_to_all | solution.py:160
  652.9 9.1 %all-to-all-start = ((f32[1,8,8,230]{3,2,0,1:T(8,128)}), f32[1,8,8,230]{3,2,0,1:T(8,128)S(1)}, u32[]{:S(2)}, u32[]{:S(2)}) async-start(f32[1,8,8,230]{3,2,0,1:T(8,128)} %convolution_bitcast_fusion.4), calls=%async_computation | async-start | bytes 131072 | tf_op jit(solution)/shard_map/while/body/eval_jaxpr/all_to_all | solution.py:159
  665.7 0.7 copy-start.1
  668.2 19.4 %collective-permute-start = (f32[1,230,256]{2,1,0:T(8,128)S(1)}, f32[1,230,256]{2,1,0:T(8,128)S(1)}, u32[]{:S(2)}, u32[]{:S(2)}) collective-permute-start(f32[1,230,256]{2,1,0:T(8,128)S(1)} %pad_maximum_fusion.2), channel_id=1, source_target_pairs={{0,8},{8,16},{16,24},{1,9},{9,17},{17,25},{2,10},{10,18},{18,26},{... | collective-permute-start | bytes 706568 | tf_op jit(solution)/shard_map/while/body/eval_jaxpr/ppermute | solution.py:14
  687.6 0.9 copy-start.2
  687.6 0.9 copy-start.3
  (15 other events, 9.7 us)
where the time goes:
time: 692 us; the launch traced here: 689 us
  blocking collectives  296 us (43%)
  starting transfers between devices  145 us (21%)
  local copies, waits for them, and re-layouts  109 us (16%)
  other arithmetic  68.2 us (10%)
  waiting for transfers between devices  30.8 us (4%)
  loops' own time  25.7 us (4%)
  matrix products  12.9 us (2%)
    all_gather x7, blocking collectives, window_work(): all_coeffs = lax.all_gather(beta_prior, 'obs', axis=2, tiled=True)  173 us
    psum x7, blocking collectives, window_work(): totals = lax.psum(statistics, 'obs')  123 us
    ppermute x7, starting transfers between devices, from_behind(): return lax.ppermute(array, axis, pairs)  95 us
    dynamic_update_slice x28, local copies, waits for them, and re-layouts, store_entry(): return lax.dynamic_update_slice_in_dim(buffer, updated, slot_index, 1)  43.8 us
    all_to_all x7, waiting for transfers between devices, window_work(): lax.all_to_all(send_rows, 'obs', split_axis=1, concat_axis=1, tiled=True)  30.8 us
    all_to_all x7, starting transfers between devices, window_work(): lax.all_to_all(send_channel, 'obs', split_axis=1, concat_axis=1, tiled=True)  26.2 us
    another operation x1, loops' own time, local(): lax.fori_loop(0, stream_count + section_count - 1, tick_step, initial)  25.7 us
    all_to_all x7, starting transfers between devices, window_work(): lax.all_to_all(send_rows, 'obs', split_axis=1, concat_axis=1, tiled=True)  23.5 us
  transfers between devices with their start and end apart: 21, of which 7 were waited for; matrix products, arithmetic and copies ran while one was open for 18% of the time, Pallas kernels for 0%

commit v1 on v0

--- a/solution.py
+++ b/solution.py
@@ -156,7 +156,12 @@
         totals = lax.psum(statistics, "obs")
         send_rows, send_channel = jax.vmap(pack_blocks)(block_sums, channel)
         got_rows, got_channel = (
-            lax.all_to_all(send_rows, "obs", split_axis=1, concat_axis=1, tiled=True),
+            jnp.concatenate(
+                lax.all_to_all(
+                    jnp.stack(jnp.split(send_rows, lax.axis_size("obs"), axis=1)), "obs", 0, 0
+                ),
+                axis=1,
+            ),
             lax.all_to_all(send_channel, "obs", split_axis=1, concat_axis=1, tiled=True),
         )
         normal = jax.vmap(unpack_blocks)(got_rows, got_channel)

time: 692 us -> 721 us (1.042)
  local copies, waits for them, and re-layouts: 109 us -> 143 us
    while x42 -> x91, local copies, waits for them, and re-layouts: 9.87 us -> 39.2 us
  transfers between devices with their start and end apart: 21 -> 21, of which waited for: 7 -> 7; matrix products, arithmetic and copies ran while one was open for 18% -> 22% of each run, Pallas kernels for 0% -> 0%
where the time goes in v1:
time: 721 us; the launch traced here: 718 us
  blocking collectives  296 us (41%)
  starting transfers between devices  145 us (20%)
  local copies, waits for them, and re-layouts  143 us (20%)
  other arithmetic  68.1 us (9%)
  waiting for transfers between devices  30.9 us (4%)
  loops' own time  25.8 us (4%)
  matrix products  8.5 us (1%)
    all_gather x7, blocking collectives, window_work(): all_coeffs = lax.all_gather(beta_prior, 'obs', axis=2, tiled=True)  173 us
    psum x7, blocking collectives, window_work(): totals = lax.psum(statistics, 'obs')  123 us
    ppermute x7, starting transfers between devices, from_behind(): return lax.ppermute(array, axis, pairs)  94.9 us
    dynamic_update_slice x28, local copies, waits for them, and re-layouts, store_entry(): return lax.dynamic_update_slice_in_dim(buffer, updated, slot_index, 1)  43.8 us
    while x91, local copies, waits for them, and re-layouts  39.2 us
    all_to_all x7, waiting for transfers between devices, window_work(): lax.all_to_all(jnp.stack(jnp.split(send_rows, lax.axis_size('obs'), axis=...  30.9 us
    all_to_all x7, starting transfers between devices, window_work(): lax.all_to_all(send_channel, 'obs', split_axis=1, concat_axis=1, tiled=True)  26.2 us
    another operation x1, loops' own time, local(): lax.fori_loop(0, stream_count + section_count - 1, tick_step, initial)  25.8 us
  transfers between devices with their start and end apart: 21, of which 7 were waited for; matrix products, arithmetic and copies ran while one was open for 22% of the time, Pallas kernels for 0%

profile of v1, /device:TPU:1, one launch (start us, length us, event | category | flops | bytes accessed | tf_op | source)
XLA Modules:
  0.0 717.6 jit_solution(7892731832164856069)
XLA Ops:
  2.9 713.8 %while.38 = (s32[]{:T(128)}, f32[1,230,256]{2,1,0:T(8,128)S(1)}, f32[1,4,20,256]{3,1,2,0:T(4,128)S(1)}, f32[1,4,210,256]{3,1,2,0:T(4,128)S(1)}, s32[]{:T(128)}, ...) while((s32[]{:T(128)}, f32[1,230,256]{2,1,0:T(8,128)S(1)}, ...), condition=%wide.region_8.10_spmd.clone.clone, body=%wide.region_0.9_spmd.sunk.clone.clone.sunk | while | flops 57759508 | bytes 13978125 | solution.py:204
  7.5 6.4 all-to-all-start.1
  16.3 24.6 %all_gather.15 = f32[1,20,2048]{2,1,0:T(8,128)S(1)} all-gather(f32[1,20,256]{2,1,0:T(8,128)S(1)} %slice.5342), channel_id=1, replica_groups=mesh['section'=4,'obs'=8] {'obs'}, dimensions={2}, use_global_device_ids=true | all-gather | bytes 184320 | tf_op jit(solution)/shard_map/while/body/eval_jaxpr/all_gather | solution.py:144
  52.6 17.5 %psum.19 = f32[1,2]{1,0:T(1,128)S(1)} all-reduce(f32[1,2]{1,0:T(1,128)S(1)} %maximum_bitcast_fusion.6), channel_id=1, replica_groups=mesh['section'=4,'obs'=8] {'obs'}, use_global_device_ids=true, to_apply=%region_7.8 | all-reduce | flops 2 | bytes 16 | tf_op jit(solution)/shard_map/while/body/eval_jaxpr/psum | solution.py:156
  76.8 4.4 all-to-all-done
  87.4 15.6 %collective-permute-start = (f32[1,230,256]{2,1,0:T(8,128)S(1)}, f32[1,230,256]{2,1,0:T(8,128)S(1)}, u32[]{:S(2)}, u32[]{:S(2)}) collective-permute-start(f32[1,230,256]{2,1,0:T(8,128)S(1)} %pad_maximum_fusion.2), channel_id=1, source_target_pairs={{0,8},{8,16},{16,24},{1,9},{9,17},{17,25},{2,10},{10,18},{18,26},{... | collective-permute-start | bytes 706568 | tf_op jit(solution)/shard_map/while/body/eval_jaxpr/ppermute | solution.py:14
  103.4 5.9 dynamic_update_slice.31
  119.7 25.2 %all_gather.15 = f32[1,20,2048]{2,1,0:T(8,128)S(1)} all-gather(f32[1,20,256]{2,1,0:T(8,128)S(1)} %slice.5342), channel_id=1, replica_groups=mesh['section'=4,'obs'=8] {'obs'}, dimensions={2}, use_global_device_ids=true | all-gather | bytes 184320 | tf_op jit(solution)/shard_map/while/body/eval_jaxpr/all_gather | solution.py:144
  156.6 17.3 %psum.19 = f32[1,2]{1,0:T(1,128)S(1)} all-reduce(f32[1,2]{1,0:T(1,128)S(1)} %maximum_bitcast_fusion.6), channel_id=1, replica_groups=mesh['section'=4,'obs'=8] {'obs'}, use_global_device_ids=true, to_apply=%region_7.8 | all-reduce | flops 2 | bytes 16 | tf_op jit(solution)/shard_map/while/body/eval_jaxpr/psum | solution.py:156
  180.6 4.4 all-to-all-done
  191.2 13.1 %collective-permute-start = (f32[1,230,256]{2,1,0:T(8,128)S(1)}, f32[1,230,256]{2,1,0:T(8,128)S(1)}, u32[]{:S(2)}, u32[]{:S(2)}) collective-permute-start(f32[1,230,256]{2,1,0:T(8,128)S(1)} %pad_maximum_fusion.2), channel_id=1, source_target_pairs={{0,8},{8,16},{16,24},{1,9},{9,17},{17,25},{2,10},{10,18},{18,26},{... | collective-permute-start | bytes 706568 | tf_op jit(solution)/shard_map/while/body/eval_jaxpr/ppermute | solution.py:14
  204.6 5.9 dynamic_update_slice.31
  220.9 24.6 %all_gather.15 = f32[1,20,2048]{2,1,0:T(8,128)S(1)} all-gather(f32[1,20,256]{2,1,0:T(8,128)S(1)} %slice.5342), channel_id=1, replica_groups=mesh['section'=4,'obs'=8] {'obs'}, dimensions={2}, use_global_device_ids=true | all-gather | bytes 184320 | tf_op jit(solution)/shard_map/while/body/eval_jaxpr/all_gather | solution.py:144
  257.3 17.5 %psum.19 = f32[1,2]{1,0:T(1,128)S(1)} all-reduce(f32[1,2]{1,0:T(1,128)S(1)} %maximum_bitcast_fusion.6), channel_id=1, replica_groups=mesh['section'=4,'obs'=8] {'obs'}, use_global_device_ids=true, to_apply=%region_7.8 | all-reduce | flops 2 | bytes 16 | tf_op jit(solution)/shard_map/while/body/eval_jaxpr/psum | solution.py:156
  292.1 13.4 %collective-permute-start = (f32[1,230,256]{2,1,0:T(8,128)S(1)}, f32[1,230,256]{2,1,0:T(8,128)S(1)}, u32[]{:S(2)}, u32[]{:S(2)}) collective-permute-start(f32[1,230,256]{2,1,0:T(8,128)S(1)} %pad_maximum_fusion.2), channel_id=1, source_target_pairs={{0,8},{8,16},{16,24},{1,9},{9,17},{17,25},{2,10},{10,18},{18,26},{... | collective-permute-start | bytes 706568 | tf_op jit(solution)/shard_map/while/body/eval_jaxpr/ppermute | solution.py:14
  305.9 5.9 dynamic_update_slice.31
  322.1 24.8 %all_gather.15 = f32[1,20,2048]{2,1,0:T(8,128)S(1)} all-gather(f32[1,20,256]{2,1,0:T(8,128)S(1)} %slice.5342), channel_id=1, replica_groups=mesh['section'=4,'obs'=8] {'obs'}, dimensions={2}, use_global_device_ids=true | all-gather | bytes 184320 | tf_op jit(solution)/shard_map/while/body/eval_jaxpr/all_gather | solution.py:144
  358.7 17.6 %psum.19 = f32[1,2]{1,0:T(1,128)S(1)} all-reduce(f32[1,2]{1,0:T(1,128)S(1)} %maximum_bitcast_fusion.6), channel_id=1, replica_groups=mesh['section'=4,'obs'=8] {'obs'}, use_global_device_ids=true, to_apply=%region_7.8 | all-reduce | flops 2 | bytes 16 | tf_op jit(solution)/shard_map/while/body/eval_jaxpr/psum | solution.py:156
  393.6 13.1 %collective-permute-start = (f32[1,230,256]{2,1,0:T(8,128)S(1)}, f32[1,230,256]{2,1,0:T(8,128)S(1)}, u32[]{:S(2)}, u32[]{:S(2)}) collective-permute-start(f32[1,230,256]{2,1,0:T(8,128)S(1)} %pad_maximum_fusion.2), channel_id=1, source_target_pairs={{0,8},{8,16},{16,24},{1,9},{9,17},{17,25},{2,10},{10,18},{18,26},{... | collective-permute-start | bytes 706568 | tf_op jit(solution)/shard_map/while/body/eval_jaxpr/ppermute | solution.py:14
  407.1 5.9 dynamic_update_slice.31
  423.4 24.9 %all_gather.15 = f32[1,20,2048]{2,1,0:T(8,128)S(1)} all-gather(f32[1,20,256]{2,1,0:T(8,128)S(1)} %slice.5342), channel_id=1, replica_groups=mesh['section'=4,'obs'=8] {'obs'}, dimensions={2}, use_global_device_ids=true | all-gather | bytes 184320 | tf_op jit(solution)/shard_map/while/body/eval_jaxpr/all_gather | solution.py:144
  460.1 17.2 %psum.19 = f32[1,2]{1,0:T(1,128)S(1)} all-reduce(f32[1,2]{1,0:T(1,128)S(1)} %maximum_bitcast_fusion.6), channel_id=1, replica_groups=mesh['section'=4,'obs'=8] {'obs'}, use_global_device_ids=true, to_apply=%region_7.8 | all-reduce | flops 2 | bytes 16 | tf_op jit(solution)/shard_map/while/body/eval_jaxpr/psum | solution.py:156
  494.5 13.4 %collective-permute-start = (f32[1,230,256]{2,1,0:T(8,128)S(1)}, f32[1,230,256]{2,1,0:T(8,128)S(1)}, u32[]{:S(2)}, u32[]{:S(2)}) collective-permute-start(f32[1,230,256]{2,1,0:T(8,128)S(1)} %pad_maximum_fusion.2), channel_id=1, source_target_pairs={{0,8},{8,16},{16,24},{1,9},{9,17},{17,25},{2,10},{10,18},{18,26},{... | collective-permute-start | bytes 706568 | tf_op jit(solution)/shard_map/while/body/eval_jaxpr/ppermute | solution.py:14
  508.3 5.9 dynamic_update_slice.31
  524.6 24.8 %all_gather.15 = f32[1,20,2048]{2,1,0:T(8,128)S(1)} all-gather(f32[1,20,256]{2,1,0:T(8,128)S(1)} %slice.5342), channel_id=1, replica_groups=mesh['section'=4,'obs'=8] {'obs'}, dimensions={2}, use_global_device_ids=true | all-gather | bytes 184320 | tf_op jit(solution)/shard_map/while/body/eval_jaxpr/all_gather | solution.py:144
  561.2 17.5 %psum.19 = f32[1,2]{1,0:T(1,128)S(1)} all-reduce(f32[1,2]{1,0:T(1,128)S(1)} %maximum_bitcast_fusion.6), channel_id=1, replica_groups=mesh['section'=4,'obs'=8] {'obs'}, use_global_device_ids=true, to_apply=%region_7.8 | all-reduce | flops 2 | bytes 16 | tf_op jit(solution)/shard_map/while/body/eval_jaxpr/psum | solution.py:156
  596.0 13.2 %collective-permute-start = (f32[1,230,256]{2,1,0:T(8,128)S(1)}, f32[1,230,256]{2,1,0:T(8,128)S(1)}, u32[]{:S(2)}, u32[]{:S(2)}) collective-permute-start(f32[1,230,256]{2,1,0:T(8,128)S(1)} %pad_maximum_fusion.2), channel_id=1, source_target_pairs={{0,8},{8,16},{16,24},{1,9},{9,17},{17,25},{2,10},{10,18},{18,26},{... | collective-permute-start | bytes 706568 | tf_op jit(solution)/shard_map/while/body/eval_jaxpr/ppermute | solution.py:14
  609.6 5.9 dynamic_update_slice.31
  625.8 24.5 %all_gather.15 = f32[1,20,2048]{2,1,0:T(8,128)S(1)} all-gather(f32[1,20,256]{2,1,0:T(8,128)S(1)} %slice.5342), channel_id=1, replica_groups=mesh['section'=4,'obs'=8] {'obs'}, dimensions={2}, use_global_device_ids=true | all-gather | bytes 184320 | tf_op jit(solution)/shard_map/while/body/eval_jaxpr/all_gather | solution.py:144
  662.0 18.0 %psum.19 = f32[1,2]{1,0:T(1,128)S(1)} all-reduce(f32[1,2]{1,0:T(1,128)S(1)} %maximum_bitcast_fusion.6), channel_id=1, replica_groups=mesh['section'=4,'obs'=8] {'obs'}, use_global_device_ids=true, to_apply=%region_7.8 | all-reduce | flops 2 | bytes 16 | tf_op jit(solution)/shard_map/while/body/eval_jaxpr/psum | solution.py:156
  697.3 13.1 %collective-permute-start = (f32[1,230,256]{2,1,0:T(8,128)S(1)}, f32[1,230,256]{2,1,0:T(8,128)S(1)}, u32[]{:S(2)}, u32[]{:S(2)}) collective-permute-start(f32[1,230,256]{2,1,0:T(8,128)S(1)} %pad_maximum_fusion.2), channel_id=1, source_target_pairs={{0,8},{8,16},{16,24},{1,9},{9,17},{17,25},{2,10},{10,18},{18,26},{... | collective-permute-start | bytes 706568 | tf_op jit(solution)/shard_map/while/body/eval_jaxpr/ppermute | solution.py:14
  710.8 5.9 dynamic_update_slice.31
  (704 shorter events, 243.6 us)
Async XLA Ops:
  2.2 0.7 copy-start.4
  2.3 0.7 copy-start.5
  7.5 64.6 %all-to-all-start.1 = ((f32[1,8,8]{2,0,1:T(1,128)}), f32[1,8,8]{2,0,1:T(1,128)S(1)}, u32[]{:S(2)}, u32[]{:S(2)}) async-start(f32[1,8,8]{2,0,1:T(1,128)} %bitcast.2500), calls=%async_computation.1 | async-start | bytes 8192 | tf_op jit(solution)/shard_map/while/body/eval_jaxpr/all_to_all | solution.py:165
  72.1 9.1 %all-to-all-start = ((f32[8,1,1,8,230]{4,3,2,1,0:T(8,128)}), f32[8,1,1,8,230]{4,3,2,1,0:T(8,128)S(1)}, u32[]{:S(2)}, u32[]{:S(2)}) async-start(f32[8,1,1,8,230]{4,3,2,1,0:T(8,128)} %constant_dynamic-update-slice_fusion.23), calls=%async_computation | async-start | bytes 131072 | tf_op jit(solution)/shard_map/while/body/eval_jaxpr/all_to_all | solution.py:160
  84.9 0.7 copy-start.1
  87.4 21.9 %collective-permute-start = (f32[1,230,256]{2,1,0:T(8,128)S(1)}, f32[1,230,256]{2,1,0:T(8,128)S(1)}, u32[]{:S(2)}, u32[]{:S(2)}) collective-permute-start(f32[1,230,256]{2,1,0:T(8,128)S(1)} %pad_maximum_fusion.2), channel_id=1, source_target_pairs={{0,8},{8,16},{16,24},{1,9},{9,17},{17,25},{2,10},{10,18},{18,26},{... | collective-permute-start | bytes 706568 | tf_op jit(solution)/shard_map/while/body/eval_jaxpr/ppermute | solution.py:14
  113.9 62.0 %all-to-all-start.1 = ((f32[1,8,8]{2,0,1:T(1,128)}), f32[1,8,8]{2,0,1:T(1,128)S(1)}, u32[]{:S(2)}, u32[]{:S(2)}) async-start(f32[1,8,8]{2,0,1:T(1,128)} %bitcast.2500), calls=%async_computation.1 | async-start | bytes 8192 | tf_op jit(solution)/shard_map/while/body/eval_jaxpr/all_to_all | solution.py:165
  175.9 9.1 %all-to-all-start = ((f32[8,1,1,8,230]{4,3,2,1,0:T(8,128)}), f32[8,1,1,8,230]{4,3,2,1,0:T(8,128)S(1)}, u32[]{:S(2)}, u32[]{:S(2)}) async-start(f32[8,1,1,8,230]{4,3,2,1,0:T(8,128)} %constant_dynamic-update-slice_fusion.23), calls=%async_computation | async-start | bytes 131072 | tf_op jit(solution)/shard_map/while/body/eval_jaxpr/all_to_all | solution.py:160
  188.7 0.7 copy-start.1
  191.2 19.4 %collective-permute-start = (f32[1,230,256]{2,1,0:T(8,128)S(1)}, f32[1,230,256]{2,1,0:T(8,128)S(1)}, u32[]{:S(2)}, u32[]{:S(2)}) collective-permute-start(f32[1,230,256]{2,1,0:T(8,128)S(1)} %pad_maximum_fusion.2), channel_id=1, source_target_pairs={{0,8},{8,16},{16,24},{1,9},{9,17},{17,25},{2,10},{10,18},{18,26},{... | collective-permute-start | bytes 706568 | tf_op jit(solution)/shard_map/while/body/eval_jaxpr/ppermute | solution.py:14
  215.2 61.7 %all-to-all-start.1 = ((f32[1,8,8]{2,0,1:T(1,128)}), f32[1,8,8]{2,0,1:T(1,128)S(1)}, u32[]{:S(2)}, u32[]{:S(2)}) async-start(f32[1,8,8]{2,0,1:T(1,128)} %bitcast.2500), calls=%async_computation.1 | async-start | bytes 8192 | tf_op jit(solution)/shard_map/while/body/eval_jaxpr/all_to_all | solution.py:165
  276.8 9.1 %all-to-all-start = ((f32[8,1,1,8,230]{4,3,2,1,0:T(8,128)}), f32[8,1,1,8,230]{4,3,2,1,0:T(8,128)S(1)}, u32[]{:S(2)}, u32[]{:S(2)}) async-start(f32[8,1,1,8,230]{4,3,2,1,0:T(8,128)} %constant_dynamic-update-slice_fusion.23), calls=%async_computation | async-start | bytes 131072 | tf_op jit(solution)/shard_map/while/body/eval_jaxpr/all_to_all | solution.py:160
  289.6 0.7 copy-start.1
  292.1 19.7 %collective-permute-start = (f32[1,230,256]{2,1,0:T(8,128)S(1)}, f32[1,230,256]{2,1,0:T(8,128)S(1)}, u32[]{:S(2)}, u32[]{:S(2)}) collective-permute-start(f32[1,230,256]{2,1,0:T(8,128)S(1)} %pad_maximum_fusion.2), channel_id=1, source_target_pairs={{0,8},{8,16},{16,24},{1,9},{9,17},{17,25},{2,10},{10,18},{18,26},{... | collective-permute-start | bytes 706568 | tf_op jit(solution)/shard_map/while/body/eval_jaxpr/ppermute | solution.py:14
  316.4 62.0 %all-to-all-start.1 = ((f32[1,8,8]{2,0,1:T(1,128)}), f32[1,8,8]{2,0,1:T(1,128)S(1)}, u32[]{:S(2)}, u32[]{:S(2)}) async-start(f32[1,8,8]{2,0,1:T(1,128)} %bitcast.2500), calls=%async_computation.1 | async-start | bytes 8192 | tf_op jit(solution)/shard_map/while/body/eval_jaxpr/all_to_all | solution.py:165
  378.4 9.1 %all-to-all-start = ((f32[8,1,1,8,230]{4,3,2,1,0:T(8,128)}), f32[8,1,1,8,230]{4,3,2,1,0:T(8,128)S(1)}, u32[]{:S(2)}, u32[]{:S(2)}) async-start(f32[8,1,1,8,230]{4,3,2,1,0:T(8,128)} %constant_dynamic-update-slice_fusion.23), calls=%async_computation | async-start | bytes 131072 | tf_op jit(solution)/shard_map/while/body/eval_jaxpr/all_to_all | solution.py:160
  391.2 0.7 copy-start.1
  393.6 19.4 %collective-permute-start = (f32[1,230,256]{2,1,0:T(8,128)S(1)}, f32[1,230,256]{2,1,0:T(8,128)S(1)}, u32[]{:S(2)}, u32[]{:S(2)}) collective-permute-start(f32[1,230,256]{2,1,0:T(8,128)S(1)} %pad_maximum_fusion.2), channel_id=1, source_target_pairs={{0,8},{8,16},{16,24},{1,9},{9,17},{17,25},{2,10},{10,18},{18,26},{... | collective-permute-start | bytes 706568 | tf_op jit(solution)/shard_map/while/body/eval_jaxpr/ppermute | solution.py:14
  417.6 61.7 %all-to-all-start.1 = ((f32[1,8,8]{2,0,1:T(1,128)}), f32[1,8,8]{2,0,1:T(1,128)S(1)}, u32[]{:S(2)}, u32[]{:S(2)}) async-start(f32[1,8,8]{2,0,1:T(1,128)} %bitcast.2500), calls=%async_computation.1 | async-start | bytes 8192 | tf_op jit(solution)/shard_map/while/body/eval_jaxpr/all_to_all | solution.py:165
  479.3 9.1 %all-to-all-start = ((f32[8,1,1,8,230]{4,3,2,1,0:T(8,128)}), f32[8,1,1,8,230]{4,3,2,1,0:T(8,128)S(1)}, u32[]{:S(2)}, u32[]{:S(2)}) async-start(f32[8,1,1,8,230]{4,3,2,1,0:T(8,128)} %constant_dynamic-update-slice_fusion.23), calls=%async_computation | async-start | bytes 131072 | tf_op jit(solution)/shard_map/while/body/eval_jaxpr/all_to_all | solution.py:160
  492.1 0.7 copy-start.1
  494.5 19.7 %collective-permute-start = (f32[1,230,256]{2,1,0:T(8,128)S(1)}, f32[1,230,256]{2,1,0:T(8,128)S(1)}, u32[]{:S(2)}, u32[]{:S(2)}) collective-permute-start(f32[1,230,256]{2,1,0:T(8,128)S(1)} %pad_maximum_fusion.2), channel_id=1, source_target_pairs={{0,8},{8,16},{16,24},{1,9},{9,17},{17,25},{2,10},{10,18},{18,26},{... | collective-permute-start | bytes 706568 | tf_op jit(solution)/shard_map/while/body/eval_jaxpr/ppermute | solution.py:14
  518.9 61.9 %all-to-all-start.1 = ((f32[1,8,8]{2,0,1:T(1,128)}), f32[1,8,8]{2,0,1:T(1,128)S(1)}, u32[]{:S(2)}, u32[]{:S(2)}) async-start(f32[1,8,8]{2,0,1:T(1,128)} %bitcast.2500), calls=%async_computation.1 | async-start | bytes 8192 | tf_op jit(solution)/shard_map/while/body/eval_jaxpr/all_to_all | solution.py:165
  580.7 9.1 %all-to-all-start = ((f32[8,1,1,8,230]{4,3,2,1,0:T(8,128)}), f32[8,1,1,8,230]{4,3,2,1,0:T(8,128)S(1)}, u32[]{:S(2)}, u32[]{:S(2)}) async-start(f32[8,1,1,8,230]{4,3,2,1,0:T(8,128)} %constant_dynamic-update-slice_fusion.23), calls=%async_computation | async-start | bytes 131072 | tf_op jit(solution)/shard_map/while/body/eval_jaxpr/all_to_all | solution.py:160
  593.5 0.7 copy-start.1
  596.0 19.5 %collective-permute-start = (f32[1,230,256]{2,1,0:T(8,128)S(1)}, f32[1,230,256]{2,1,0:T(8,128)S(1)}, u32[]{:S(2)}, u32[]{:S(2)}) collective-permute-start(f32[1,230,256]{2,1,0:T(8,128)S(1)} %pad_maximum_fusion.2), channel_id=1, source_target_pairs={{0,8},{8,16},{16,24},{1,9},{9,17},{17,25},{2,10},{10,18},{18,26},{... | collective-permute-start | bytes 706568 | tf_op jit(solution)/shard_map/while/body/eval_jaxpr/ppermute | solution.py:14
  620.1 62.0 %all-to-all-start.1 = ((f32[1,8,8]{2,0,1:T(1,128)}), f32[1,8,8]{2,0,1:T(1,128)S(1)}, u32[]{:S(2)}, u32[]{:S(2)}) async-start(f32[1,8,8]{2,0,1:T(1,128)} %bitcast.2500), calls=%async_computation.1 | async-start | bytes 8192 | tf_op jit(solution)/shard_map/while/body/eval_jaxpr/all_to_all | solution.py:165
  682.1 9.1 %all-to-all-start = ((f32[8,1,1,8,230]{4,3,2,1,0:T(8,128)}), f32[8,1,1,8,230]{4,3,2,1,0:T(8,128)S(1)}, u32[]{:S(2)}, u32[]{:S(2)}) async-start(f32[8,1,1,8,230]{4,3,2,1,0:T(8,128)} %constant_dynamic-update-slice_fusion.23), calls=%async_computation | async-start | bytes 131072 | tf_op jit(solution)/shard_map/while/body/eval_jaxpr/all_to_all | solution.py:160
  694.8 0.7 copy-start.1
  697.3 19.4 %collective-permute-start = (f32[1,230,256]{2,1,0:T(8,128)S(1)}, f32[1,230,256]{2,1,0:T(8,128)S(1)}, u32[]{:S(2)}, u32[]{:S(2)}) collective-permute-start(f32[1,230,256]{2,1,0:T(8,128)S(1)} %pad_maximum_fusion.2), channel_id=1, source_target_pairs={{0,8},{8,16},{16,24},{1,9},{9,17},{17,25},{2,10},{10,18},{18,26},{... | collective-permute-start | bytes 706568 | tf_op jit(solution)/shard_map/while/body/eval_jaxpr/ppermute | solution.py:14
  716.7 0.9 copy-start.2
  716.7 0.9 copy-start.3
  (15 other events, 9.7 us)
